TPU v7x, 32 devices: a whole 2x2x4 slice. The times are simulated.
32 devices in a mesh: groups: 2 (over x), segment: 2 (over core), block: 8 (over z, y).
Axes of the slice: x: 2, y: 2, z: 4, core: 2. Of those that a mesh axis runs over, the one named last changes fastest.
Arguments:
- tokens: float32 [1024, 16384], P(('groups', 'segment'), 'block'), parts along dimension 0, may hold values from -32 to 32
- gains: float32 [2, 2, 16384], P('segment', None, 'block'), may hold values from 0.1 to 1.9
- right_factors: float32 [2, 2, 128, 128, 128], P('segment', None, 'block'), may hold values from -0.5 to 0.5
- left_factors: float32 [2, 2, 128, 128, 128], P('segment', None, 'block'), may hold values from -0.5 to 0.5
Outputs:
- output: float32 [1024, 16384], P(('groups', 'segment'), 'block'), parts along dimension 0
There are 2 independent parts, one for each index of `groups`. A program takes and returns all parts, laid end to end along the dimension named above; an argument that names none is the same for every part. Nothing has to cross between parts.
All inputs are finite; a program needn't handle non-finite values.
Results may differ from a plain program's by a relative error of at most 0.0003.
Values sent between devices are 32-bit elements; how exact they have to be, the bound alone decides.
A program may use at most 64 MiB of HBM per device.

v0:
```python
import jax
import jax.numpy as jnp
from jax import lax
from jax.sharding import PartitionSpec as P

D = 16384
epsilon = 1e-06
exact = lax.Precision.HIGH


def shifted(block, axis, distance):
    devices = range(lax.axis_size(axis))
    route = [((i - distance) % len(devices), i) for i in devices]
    return lax.ppermute(block, axis, route)


def apply_layer(current, gain_row, right_part, left_part):
    blocks_here = right_part.shape[0]
    block_size = right_part.shape[1]
    width_here, token_count = current.shape
    partial_squares = jnp.sum(current * current, axis=0)
    devices = lax.axis_size("block")
    copies = jnp.broadcast_to(partial_squares, (devices, token_count))
    sum_squares = lax.all_to_all(copies, "block", 0, 0, tiled=True).sum(axis=0)
    normed = current * lax.rsqrt(sum_squares / D + epsilon)[None, :] * gain_row[:, None]
    inner = jnp.einsum(
        "bit,bij->bjt",
        normed.reshape(blocks_here, block_size, token_count),
        right_part,
        precision=exact,
    )
    combined = jnp.einsum(
        "bjt,jbc->cjt",
        lax.all_to_all(inner, "block", split_axis=1, concat_axis=0, tiled=True),
        left_part,
        precision=exact,
    )
    mixed = lax.all_to_all(combined, "block", split_axis=0, concat_axis=1, tiled=True)
    return current + mixed.reshape(width_here, token_count) * jax.nn.silu(normed)


def body(tokens, gains, right_factors, left_factors):
    current = tokens.T
    rounds = right_factors.shape[1]
    segment_index = lax.axis_index("segment")
    own = (gains[0], right_factors[0], left_factors[0])
    other = [[shifted(part[r], "segment", 1) for part in own] for r in range(rounds)]
    for layer_index in range(2 * rounds):
        section, r = (layer_index % 2, layer_index // 2)
        chosen = [
            jnp.where(segment_index == section, mine[r], theirs)
            for mine, theirs in zip(own, other[r])
        ]
        current = apply_layer(current, *chosen)
    return current.T


def solution(mesh):
    placed = (
        P(("groups", "segment"), "block"),
        P("segment", None, "block"),
        P("segment", None, "block", None, None),
        P("segment", None, "block", None, None),
    )
    return jax.shard_map(
        body,
        mesh=mesh,
        in_specs=placed,
        out_specs=P(("groups", "segment"), "block"),
        check_vma=False,
    )
```

profile of v0, /device:TPU:0, one launch (start us, length us, event | category | flops | bytes accessed | tf_op | source)
XLA Modules:
  0.0 513.8 jit_solution(17633843209926145523)
XLA Ops:
  1.3 3.1 slice_bitcast_fusion
  7.3 7.3 %all-to-all-start = ((f32[8,1,256]{2,1,0:T(1,128)}), f32[8,1,256]{2,1,0:T(1,128)S(1)}, u32[]{:S(2)}, u32[]{:S(2)}) async-start(f32[8,1,256]{2,1,0:T(1,128)} %broadcast_in_dim.8), calls=%async_computation | async-start | bytes 16384 | tf_op jit(solution)/shard_map/all_to_all | solution.py:24
  14.6 6.5 %all-to-all-done = f32[8,1,256]{2,1,0:T(1,128)S(1)} async-done(((f32[8,1,256]{2,1,0:T(1,128)}), f32[8,1,256]{2,1,0:T(1,128)S(1)}, u32[]{:S(2)}, u32[]{:S(2)}) %all-to-all-start) | async-done | bytes 8224 | tf_op jit(solution)/shard_map/all_to_all | solution.py:24
  23.9 2.5 copy.120
  26.5 4.4 all-to-all-start.1
  30.8 3.1 slice_bitcast_fusion.1
  33.9 44.2 %all-to-all-done.1 = f32[16,128,256]{2,0,1:T(8,128)} async-done(((f32[16,128,256]{2,0,1:T(8,128)}), f32[16,128,256]{2,0,1:T(8,128)}, u32[]{:S(2)}, u32[]{:S(2)}) %all-to-all-start.1) | async-done | bytes 2097184 | tf_op jit(solution)/shard_map/all_to_all | solution.py:34
  82.8 53.1 %all_to_all.156 = f32[128,16,256]{2,1,0:T(8,128)S(1)} all-to-all(f32[128,16,256]{2,1,0:T(8,128)S(1)} %copy.123), channel_id=1, replica_groups=mesh['groups'=2,'segment'=2,'block'=8] {'block'}, dimensions={0} | all-to-all | bytes 4194304 | tf_op jit(solution)/shard_map/all_to_all | solution.py:38
  138.3 10.0 %all_to_all.157 = f32[8,1,256]{2,1,0:T(1,128)S(1)} all-to-all(f32[8,1,256]{2,1,0:T(1,128)S(1)} %broadcast_in_dim.9), channel_id=1, replica_groups=mesh['groups'=2,'segment'=2,'block'=8] {'block'}, dimensions={0} | all-to-all | bytes 16384 | tf_op jit(solution)/shard_map/all_to_all | solution.py:24
  153.0 49.9 %all_to_all.158 = f32[16,128,256]{2,0,1:T(8,128)S(1)} all-to-all(f32[16,128,256]{2,0,1:T(8,128)S(1)} %copy.127), channel_id=1, replica_groups=mesh['groups'=2,'segment'=2,'block'=8] {'block'}, dimensions={1} | all-to-all | bytes 4194304 | tf_op jit(solution)/shard_map/all_to_all | solution.py:34
  204.5 2.4 convolution_bitcast_fusion.2
  207.0 2.6 copy.130
  209.5 3.6 all-to-all-start.5
  213.7 46.0 %all-to-all-done.5 = f32[128,16,256]{2,1,0:T(8,128)S(1)} async-done(((f32[128,16,256]{2,1,0:T(8,128)}), f32[128,16,256]{2,1,0:T(8,128)S(1)}, u32[]{:S(2)}, u32[]{:S(2)}) %all-to-all-start.5) | async-done | bytes 2097184 | tf_op jit(solution)/shard_map/all_to_all | solution.py:38
  262.8 3.4 all-to-all-start.6
  266.2 6.5 %all-to-all-done.6 = f32[8,1,256]{2,1,0:T(1,128)S(1)} async-done(((f32[8,1,256]{2,1,0:T(1,128)}), f32[8,1,256]{2,1,0:T(1,128)S(1)}, u32[]{:S(2)}, u32[]{:S(2)}) %all-to-all-start.6) | async-done | bytes 8224 | tf_op jit(solution)/shard_map/all_to_all | solution.py:24
  275.6 2.5 copy.134
  278.1 4.4 all-to-all-start.7
  282.5 47.2 %all-to-all-done.7 = f32[16,128,256]{2,0,1:T(8,128)} async-done(((f32[16,128,256]{2,0,1:T(8,128)}), f32[16,128,256]{2,0,1:T(8,128)}, u32[]{:S(2)}, u32[]{:S(2)}) %all-to-all-start.7) | async-done | bytes 2097184 | tf_op jit(solution)/shard_map/all_to_all | solution.py:34
  334.4 53.1 %all_to_all.159 = f32[128,16,256]{2,1,0:T(8,128)S(1)} all-to-all(f32[128,16,256]{2,1,0:T(8,128)S(1)} %copy.137), channel_id=1, replica_groups=mesh['groups'=2,'segment'=2,'block'=8] {'block'}, dimensions={0} | all-to-all | bytes 4194304 | tf_op jit(solution)/shard_map/all_to_all | solution.py:38
  389.9 10.0 %all_to_all.160 = f32[8,1,256]{2,1,0:T(1,128)S(1)} all-to-all(f32[8,1,256]{2,1,0:T(1,128)S(1)} %broadcast_in_dim.11), channel_id=1, replica_groups=mesh['groups'=2,'segment'=2,'block'=8] {'block'}, dimensions={0} | all-to-all | bytes 16384 | tf_op jit(solution)/shard_map/all_to_all | solution.py:24
  404.7 49.9 %all_to_all.161 = f32[16,128,256]{2,0,1:T(8,128)S(1)} all-to-all(f32[16,128,256]{2,0,1:T(8,128)S(1)} %copy.141), channel_id=1, replica_groups=mesh['groups'=2,'segment'=2,'block'=8] {'block'}, dimensions={1} | all-to-all | bytes 4194304 | tf_op jit(solution)/shard_map/all_to_all | solution.py:34
  456.1 2.4 convolution_bitcast_fusion
  459.8 49.8 %all_to_all.162 = f32[128,16,256]{2,1,0:T(8,128)S(1)} all-to-all(f32[128,16,256]{2,1,0:T(8,128)S(1)} %copy.144), channel_id=1, replica_groups=mesh['groups'=2,'segment'=2,'block'=8] {'block'}, dimensions={0} | all-to-all | bytes 4194304 | tf_op jit(solution)/shard_map/all_to_all | solution.py:38
  (77 shorter events, 45.5 us)
Async XLA Ops:
  0.8 13.8 %collective-permute-start.2 = (f32[2048]{0:T(1024)S(1)}, f32[2048]{0:T(1024)S(1)}, u32[]{:S(2)}, u32[]{:S(2)}) collective-permute-start(f32[2048]{0:T(1024)S(1)} %bitcast.130), channel_id=1, source_target_pairs={{8,0},{0,8},{9,1},{1,9},{10,2},{2,10},{11,3},{3,11},{12,4},{4,12},... | collective-permute-start | bytes 24584 | tf_op jit(solution)/shard_map/ppermute | solution.py:14
  4.4 17.1 %collective-permute-start.1 = (f32[16,128,128]{2,1,0:T(8,128)}, f32[16,128,128]{2,1,0:T(8,128)S(1)}, u32[]{:S(2)}, u32[]{:S(2)}) collective-permute-start(f32[16,128,128]{2,1,0:T(8,128)} %get-tuple-element.14), channel_id=1, source_target_pairs={{8,0},{0,8},{9,1},{1,9},{10,2},{2,10},{11,3},{3,11},{12,4},{4,12},... | collective-permute-start | bytes 3145736 | tf_op jit(solution)/shard_map/ppermute | solution.py:14
  7.3 13.8 %all-to-all-start = ((f32[8,1,256]{2,1,0:T(1,128)}), f32[8,1,256]{2,1,0:T(1,128)S(1)}, u32[]{:S(2)}, u32[]{:S(2)}) async-start(f32[8,1,256]{2,1,0:T(1,128)} %broadcast_in_dim.8), calls=%async_computation | async-start | bytes 16384 | tf_op jit(solution)/shard_map/all_to_all | solution.py:24
  21.1 1.6 copy-start.1
  26.5 51.6 %all-to-all-start.1 = ((f32[16,128,256]{2,0,1:T(8,128)}), f32[16,128,256]{2,0,1:T(8,128)}, u32[]{:S(2)}, u32[]{:S(2)}) async-start(f32[16,128,256]{2,0,1:T(8,128)} %copy.120), calls=%async_computation.1 | async-start | bytes 4194304 | tf_op jit(solution)/shard_map/all_to_all | solution.py:34
  33.9 46.1 %collective-permute-start = (f32[16,128,128]{2,1,0:T(8,128)}, f32[16,128,128]{2,1,0:T(8,128)}, u32[]{:S(2)}, u32[]{:S(2)}) collective-permute-start(f32[16,128,128]{2,1,0:T(8,128)} %get-tuple-element.12), channel_id=1, source_target_pairs={{8,0},{0,8},{9,1},{1,9},{10,2},{2,10},{11,3},{3,11},{12,4},{4,12},... | collective-permute-start | bytes 3145736 | tf_op jit(solution)/shard_map/ppermute | solution.py:14
  78.1 2.2 copy-start.5
  148.4 2.2 copy-start.2
  202.9 1.6 copy-start.6
  209.5 50.2 %all-to-all-start.5 = ((f32[128,16,256]{2,1,0:T(8,128)}), f32[128,16,256]{2,1,0:T(8,128)S(1)}, u32[]{:S(2)}, u32[]{:S(2)}) async-start(f32[128,16,256]{2,1,0:T(8,128)} %copy.130), calls=%async_computation.5 | async-start | bytes 4194304 | tf_op jit(solution)/shard_map/all_to_all | solution.py:38
  213.1 53.1 %collective-permute-start.5 = (f32[2048]{0:T(1024)S(1)}, f32[2048]{0:T(1024)S(1)}, u32[]{:S(2)}, u32[]{:S(2)}) collective-permute-start(f32[2048]{0:T(1024)S(1)} %bitcast.128), channel_id=1, source_target_pairs={{8,0},{0,8},{9,1},{1,9},{10,2},{2,10},{11,3},{3,11},{12,4},{4,12},... | collective-permute-start | bytes 24584 | tf_op jit(solution)/shard_map/ppermute | solution.py:14
  213.2 59.9 %collective-permute-start.4 = (f32[16,128,128]{2,1,0:T(8,128)}, f32[16,128,128]{2,1,0:T(8,128)S(1)}, u32[]{:S(2)}, u32[]{:S(2)}) collective-permute-start(f32[16,128,128]{2,1,0:T(8,128)} %get-tuple-element.13), channel_id=1, source_target_pairs={{8,0},{0,8},{9,1},{1,9},{10,2},{2,10},{11,3},{3,11},{12,4},{4,12},... | collective-permute-start | bytes 3145736 | tf_op jit(solution)/shard_map/ppermute | solution.py:14
  259.7 1.6 copy-start
  262.8 9.9 %all-to-all-start.6 = ((f32[8,1,256]{2,1,0:T(1,128)}), f32[8,1,256]{2,1,0:T(1,128)S(1)}, u32[]{:S(2)}, u32[]{:S(2)}) async-start(f32[8,1,256]{2,1,0:T(1,128)} %broadcast_in_dim.10), calls=%async_computation.6 | async-start | bytes 16384 | tf_op jit(solution)/shard_map/all_to_all | solution.py:24
  272.8 1.6 copy-start.3
  278.1 51.6 %all-to-all-start.7 = ((f32[16,128,256]{2,0,1:T(8,128)}), f32[16,128,256]{2,0,1:T(8,128)}, u32[]{:S(2)}, u32[]{:S(2)}) async-start(f32[16,128,256]{2,0,1:T(8,128)} %copy.134), calls=%async_computation.7 | async-start | bytes 4194304 | tf_op jit(solution)/shard_map/all_to_all | solution.py:34
  282.5 49.2 %collective-permute-start.3 = (f32[16,128,128]{2,1,0:T(8,128)}, f32[16,128,128]{2,1,0:T(8,128)}, u32[]{:S(2)}, u32[]{:S(2)}) collective-permute-start(f32[16,128,128]{2,1,0:T(8,128)} %get-tuple-element.11), channel_id=1, source_target_pairs={{8,0},{0,8},{9,1},{1,9},{10,2},{2,10},{11,3},{3,11},{12,4},{4,12},... | collective-permute-start | bytes 3145736 | tf_op jit(solution)/shard_map/ppermute | solution.py:14
  329.7 2.2 copy-start.7
  400.0 2.2 copy-start.4
  454.6 1.6 copy-start.8
  509.6 1.6 copy-start.9
where the time goes:
time: 515 us; the launch traced here: 514 us
  blocking collectives  276 us (54%)
  waiting for transfers between devices  150 us (29%)
  local copies, waits for them, and re-layouts  39.6 us (8%)
  starting transfers between devices  24.2 us (5%)
  matrix products  12.1 us (2%)
  other arithmetic  11.3 us (2%)
    all_to_all x3, blocking collectives, apply_layer(): lax.all_to_all(combined, 'block', split_axis=0, concat_axis=1, tiled=True)  156 us
    all_to_all x2, blocking collectives, apply_layer(): lax.all_to_all(inner, 'block', split_axis=1, concat_axis=0, tiled=True)  99.8 us
    all_to_all x2, waiting for transfers between devices, apply_layer(): lax.all_to_all(inner, 'block', split_axis=1, concat_axis=0, tiled=True)  91.3 us
    all_to_all x1, waiting for transfers between devices, apply_layer(): lax.all_to_all(combined, 'block', split_axis=0, concat_axis=1, tiled=True)  46 us
    all_to_all x2, blocking collectives, apply_layer(): sum_squares = lax.all_to_all(copies, 'block', 0, 0, tiled=True).sum(axis=0)  20 us
    all_to_all x2, waiting for transfers between devices, apply_layer(): sum_squares = lax.all_to_all(copies, 'block', 0, 0, tiled=True).sum(axis=0)  13 us
    all_to_all x2, starting transfers between devices, apply_layer(): sum_squares = lax.all_to_all(copies, 'block', 0, 0, tiled=True).sum(axis=0)  10.7 us
    unnamed x21, local copies, waits for them, and re-layouts  10.7 us
  transfers between devices with their start and end apart: 11, of which 5 were waited for; matrix products, arithmetic and copies ran while one was open for 3% of the time, Pallas kernels for 0%

commit v1 on v0

--- a/solution.py
+++ b/solution.py
@@ -6,6 +6,28 @@
 D = 16384
 epsilon = 1e-06
 exact = lax.Precision.HIGH
+
+
+def in_blocks(array, dim, size):
+    before, after = (array.shape[:dim], array.shape[dim + 1 :])
+    return jnp.moveaxis(array.reshape(*before, size, -1, *after), dim, 0)
+
+
+def laid_out(blocks, dim):
+    blocks = jnp.moveaxis(blocks, 0, dim)
+    shape = blocks.shape
+    return blocks.reshape(*shape[:dim], shape[dim] * shape[dim + 1], *shape[dim + 2 :])
+
+
+def pairwise_exchange(value, axis, split_dim, concat_dim):
+    size, index = (lax.axis_size(axis), lax.axis_index(axis))
+    parts = in_blocks(value, split_dim, size)
+    outs = [parts[index]]
+    for step in range(1, size):
+        sent = parts[index ^ step]
+        outs.append(lax.ppermute(sent, axis, [(i, i ^ step) for i in range(size)]))
+    parts = jnp.stack(outs)[index ^ jnp.arange(size)]
+    return laid_out(parts, concat_dim)
 
 
 def shifted(block, axis, distance):
@@ -35,7 +57,7 @@
         left_part,
         precision=exact,
     )
-    mixed = lax.all_to_all(combined, "block", split_axis=0, concat_axis=1, tiled=True)
+    mixed = pairwise_exchange(combined, "block", 0, 1)
     return current + mixed.reshape(width_here, token_count) * jax.nn.silu(normed)
 
 

time: 515 us -> 531 us (1.031)
  blocking collectives: 276 us -> 134 us
  waiting for transfers between devices: 150 us -> 224 us
  starting transfers between devices: 24.2 us -> 68.5 us
  local copies, waits for them, and re-layouts: 39.6 us -> 77.1 us
    all_to_all x3 -> x0, blocking collectives: 156 us -> none  [apply_layer(): lax.all_to_all(combined, 'block', split_axis=0, concat_axis=1, tiled=True)]
    ppermute x0 -> x28, waiting for transfers between devices: none -> 120 us  [pairwise_exchange(): outs.append(lax.ppermute(sent, axis, [(i, i ^ step) for i in range(size)]))]
    all_to_all x1 -> x0, waiting for transfers between devices: 46 us -> none  [apply_layer(): lax.all_to_all(combined, 'block', split_axis=0, concat_axis=1, tiled=True)]
    ppermute x0 -> x28, starting transfers between devices: none -> 38.5 us  [pairwise_exchange(): outs.append(lax.ppermute(sent, axis, [(i, i ^ step) for i in range(size)]))]
    unnamed x21 -> x49, local copies, waits for them, and re-layouts: 10.7 us -> 31.5 us
    all_to_all x2, blocking collectives: 20 us -> 35.1 us  [apply_layer(): sum_squares = lax.all_to_all(copies, 'block', 0, 0, tiled=True).sum(axis=0)]
    gather x0 -> x4, local copies, waits for them, and re-layouts: none -> 11.8 us  [pairwise_exchange(): parts = jnp.stack(outs)[index ^ jnp.arange(size)]]
    all_to_all x2, starting transfers between devices: 10.7 us -> 19.8 us  [apply_layer(): sum_squares = lax.all_to_all(copies, 'block', 0, 0, tiled=True).sum(axis=0)]
  transfers between devices with their start and end apart: 11 -> 38, of which waited for: 5 -> 18; matrix products, arithmetic and copies ran while one was open for 3% -> 8% of each run, Pallas kernels for 0% -> 0%
where the time goes in v1:
time: 531 us; the launch traced here: 527 us
  waiting for transfers between devices  224 us (42%)
  blocking collectives  134 us (25%)
  local copies, waits for them, and re-layouts  77.1 us (15%)
  starting transfers between devices  68.5 us (13%)
  matrix products  12.1 us (2%)
  other arithmetic  11.3 us (2%)
    ppermute x28, waiting for transfers between devices, pairwise_exchange(): outs.append(lax.ppermute(sent, axis, [(i, i ^ step) for i in range(size)]))  120 us
    all_to_all x2, blocking collectives, apply_layer(): lax.all_to_all(inner, 'block', split_axis=1, concat_axis=0, tiled=True)  98.7 us
    all_to_all x2, waiting for transfers between devices, apply_layer(): lax.all_to_all(inner, 'block', split_axis=1, concat_axis=0, tiled=True)  91.1 us
    ppermute x28, starting transfers between devices, pairwise_exchange(): outs.append(lax.ppermute(sent, axis, [(i, i ^ step) for i in range(size)]))  38.5 us
    all_to_all x2, blocking collectives, apply_layer(): sum_squares = lax.all_to_all(copies, 'block', 0, 0, tiled=True).sum(axis=0)  35.1 us
    unnamed x49, local copies, waits for them, and re-layouts  31.5 us
    all_to_all x2, starting transfers between devices, apply_layer(): sum_squares = lax.all_to_all(copies, 'block', 0, 0, tiled=True).sum(axis=0)  19.8 us
    all_to_all x2, waiting for transfers between devices, apply_layer(): sum_squares = lax.all_to_all(copies, 'block', 0, 0, tiled=True).sum(axis=0)  13 us
  transfers between devices with their start and end apart: 38, of which 18 were waited for; matrix products, arithmetic and copies ran while one was open for 8% of the time, Pallas kernels for 0%

profile of v1, /device:TPU:0, one launch (start us, length us, event | category | flops | bytes accessed | tf_op | source)
XLA Modules:
  0.0 527.0 jit_solution(10918746640089043965)
XLA Ops:
  7.3 7.3 %all-to-all-start = ((f32[8,1,256]{2,1,0:T(1,128)}), f32[8,1,256]{2,1,0:T(1,128)S(1)}, u32[]{:S(2)}, u32[]{:S(2)}) async-start(f32[8,1,256]{2,1,0:T(1,128)} %broadcast_in_dim.8), calls=%async_computation | async-start | bytes 16384 | tf_op jit(solution)/shard_map/all_to_all | solution.py:46
  14.6 6.5 %all-to-all-done = f32[8,1,256]{2,1,0:T(1,128)S(1)} async-done(((f32[8,1,256]{2,1,0:T(1,128)}), f32[8,1,256]{2,1,0:T(1,128)S(1)}, u32[]{:S(2)}, u32[]{:S(2)}) %all-to-all-start) | async-done | bytes 8224 | tf_op jit(solution)/shard_map/all_to_all | solution.py:46
  26.5 4.4 all-to-all-start.1
  33.9 44.2 %all-to-all-done.1 = f32[16,128,256]{2,0,1:T(8,128)} async-done(((f32[16,128,256]{2,0,1:T(8,128)}), f32[16,128,256]{2,0,1:T(8,128)}, u32[]{:S(2)}, u32[]{:S(2)}) %all-to-all-start.1) | async-done | bytes 2097184 | tf_op jit(solution)/shard_map/all_to_all | solution.py:56
  87.3 3.8 collective-permute-start.7
  93.6 7.5 %collective-permute-done.4 = f32[16,16,256]{2,1,0:T(8,128)S(1)} collective-permute-done((f32[16,16,256]{2,1,0:T(8,128)S(1)}, f32[16,16,256]{2,1,0:T(8,128)S(1)}, u32[]{:S(2)}, u32[]{:S(2)}) %collective-permute-start.4) | collective-permute-done | bytes 262176 | tf_op jit(solution)/shard_map/ppermute | solution.py:28
  105.9 20.2 %collective-permute-done.7 = f32[16,16,256]{2,1,0:T(8,128)S(1)} collective-permute-done((f32[16,16,256]{2,1,0:T(8,128)S(1)}, f32[16,16,256]{2,1,0:T(8,128)S(1)}, u32[]{:S(2)}, u32[]{:S(2)}) %collective-permute-start.7) | collective-permute-done | bytes 262176 | tf_op jit(solution)/shard_map/ppermute | solution.py:28
  128.3 3.6 gather_fusion
  135.9 17.5 %all_to_all.96 = f32[8,1,256]{2,1,0:T(1,128)S(1)} all-to-all(f32[8,1,256]{2,1,0:T(1,128)S(1)} %broadcast_in_dim.9), channel_id=1, replica_groups=mesh['groups'=2,'segment'=2,'block'=8] {'block'}, dimensions={0} | all-to-all | bytes 16384 | tf_op jit(solution)/shard_map/all_to_all | solution.py:46
  158.1 49.3 %all_to_all.97 = f32[16,128,256]{2,0,1:T(8,128)S(1)} all-to-all(f32[16,128,256]{2,0,1:T(8,128)S(1)} %copy.214), channel_id=1, replica_groups=mesh['groups'=2,'segment'=2,'block'=8] {'block'}, dimensions={1} | all-to-all | bytes 4194304 | tf_op jit(solution)/shard_map/all_to_all | solution.py:56
  220.0 9.5 %collective-permute-done.11 = f32[16,16,256]{2,1,0:T(8,128)S(1)} collective-permute-done((f32[16,16,256]{2,1,0:T(8,128)S(1)}, f32[16,16,256]{2,1,0:T(8,128)S(1)}, u32[]{:S(2)}, u32[]{:S(2)}) %collective-permute-start.11) | collective-permute-done | bytes 262176 | tf_op jit(solution)/shard_map/ppermute | solution.py:28
  235.6 4.1 collective-permute-start.16
  240.4 16.2 %collective-permute-done.14 = f32[16,16,256]{2,1,0:T(8,128)S(1)} collective-permute-done((f32[16,16,256]{2,1,0:T(8,128)S(1)}, f32[16,16,256]{2,1,0:T(8,128)S(1)}, u32[]{:S(2)}, u32[]{:S(2)}) %collective-permute-start.14) | collective-permute-done | bytes 262176 | tf_op jit(solution)/shard_map/ppermute | solution.py:28
  264.1 12.6 %all-to-all-start.4 = ((f32[8,1,256]{2,1,0:T(1,128)}), f32[8,1,256]{2,1,0:T(1,128)S(1)}, u32[]{:S(2)}, u32[]{:S(2)}) async-start(f32[8,1,256]{2,1,0:T(1,128)} %broadcast_in_dim.10), calls=%async_computation.4 | async-start | bytes 16384 | tf_op jit(solution)/shard_map/all_to_all | solution.py:46
  276.7 6.5 %all-to-all-done.4 = f32[8,1,256]{2,1,0:T(1,128)S(1)} async-done(((f32[8,1,256]{2,1,0:T(1,128)}), f32[8,1,256]{2,1,0:T(1,128)S(1)}, u32[]{:S(2)}, u32[]{:S(2)}) %all-to-all-start.4) | async-done | bytes 8224 | tf_op jit(solution)/shard_map/all_to_all | solution.py:46
  288.6 4.6 all-to-all-start.5
  293.3 47.0 %all-to-all-done.5 = f32[16,128,256]{2,0,1:T(8,128)} async-done(((f32[16,128,256]{2,0,1:T(8,128)}), f32[16,128,256]{2,0,1:T(8,128)}, u32[]{:S(2)}, u32[]{:S(2)}) %all-to-all-start.5) | async-done | bytes 2097184 | tf_op jit(solution)/shard_map/all_to_all | solution.py:56
  355.7 7.5 %collective-permute-done.21 = f32[16,16,256]{2,1,0:T(8,128)S(1)} collective-permute-done((f32[16,16,256]{2,1,0:T(8,128)S(1)}, f32[16,16,256]{2,1,0:T(8,128)S(1)}, u32[]{:S(2)}, u32[]{:S(2)}) %collective-permute-start.21) | collective-permute-done | bytes 262176 | tf_op jit(solution)/shard_map/ppermute | solution.py:28
  368.2 20.1 %collective-permute-done.24 = f32[16,16,256]{2,1,0:T(8,128)S(1)} collective-permute-done((f32[16,16,256]{2,1,0:T(8,128)S(1)}, f32[16,16,256]{2,1,0:T(8,128)S(1)}, u32[]{:S(2)}, u32[]{:S(2)}) %collective-permute-start.24) | collective-permute-done | bytes 262176 | tf_op jit(solution)/shard_map/ppermute | solution.py:28
  398.0 17.6 %all_to_all.98 = f32[8,1,256]{2,1,0:T(1,128)S(1)} all-to-all(f32[8,1,256]{2,1,0:T(1,128)S(1)} %broadcast_in_dim.11), channel_id=1, replica_groups=mesh['groups'=2,'segment'=2,'block'=8] {'block'}, dimensions={0} | all-to-all | bytes 16384 | tf_op jit(solution)/shard_map/all_to_all | solution.py:46
  420.4 49.3 %all_to_all.99 = f32[16,128,256]{2,0,1:T(8,128)S(1)} all-to-all(f32[16,128,256]{2,0,1:T(8,128)S(1)} %copy.242), channel_id=1, replica_groups=mesh['groups'=2,'segment'=2,'block'=8] {'block'}, dimensions={1} | all-to-all | bytes 4194304 | tf_op jit(solution)/shard_map/all_to_all | solution.py:56
  485.7 5.5 %collective-permute-done.28 = f32[16,16,256]{2,1,0:T(8,128)S(1)} collective-permute-done((f32[16,16,256]{2,1,0:T(8,128)S(1)}, f32[16,16,256]{2,1,0:T(8,128)S(1)}, u32[]{:S(2)}, u32[]{:S(2)}) %collective-permute-start.28) | collective-permute-done | bytes 262176 | tf_op jit(solution)/shard_map/ppermute | solution.py:28
  494.7 17.1 %collective-permute-done.30 = f32[16,16,256]{2,1,0:T(8,128)S(1)} collective-permute-done((f32[16,16,256]{2,1,0:T(8,128)S(1)}, f32[16,16,256]{2,1,0:T(8,128)S(1)}, u32[]{:S(2)}, u32[]{:S(2)}) %collective-permute-start.30) | collective-permute-done | bytes 262176 | tf_op jit(solution)/shard_map/ppermute | solution.py:28
  512.5 5.9 %collective-permute-done.31 = f32[16,16,256]{2,1,0:T(8,128)S(1)} collective-permute-done((f32[16,16,256]{2,1,0:T(8,128)S(1)}, f32[16,16,256]{2,1,0:T(8,128)S(1)}, u32[]{:S(2)}, u32[]{:S(2)}) %collective-permute-start.31) | collective-permute-done | bytes 262176 | tf_op jit(solution)/shard_map/ppermute | solution.py:28
  (194 shorter events, 138.7 us)
Async XLA Ops:
  26.5 51.6 %all-to-all-start.1 = ((f32[16,128,256]{2,0,1:T(8,128)}), f32[16,128,256]{2,0,1:T(8,128)}, u32[]{:S(2)}, u32[]{:S(2)}) async-start(f32[16,128,256]{2,0,1:T(8,128)} %copy.200), calls=%async_computation.1 | async-start | bytes 4194304 | tf_op jit(solution)/shard_map/all_to_all | solution.py:56
  33.9 46.1 %collective-permute-start = (f32[16,128,128]{2,1,0:T(8,128)}, f32[16,128,128]{2,1,0:T(8,128)}, u32[]{:S(2)}, u32[]{:S(2)}) collective-permute-start(f32[16,128,128]{2,1,0:T(8,128)} %get-tuple-element.28), channel_id=1, source_target_pairs={{8,0},{0,8},{9,1},{1,9},{10,2},{2,10},{11,3},{3,11},{12,4},{4,12},... | collective-permute-start | bytes 3145736 | tf_op jit(solution)/shard_map/ppermute | solution.py:36
  84.7 19.8 %collective-permute-start.5 = (f32[16,16,256]{2,1,0:T(8,128)S(1)}, f32[16,16,256]{2,1,0:T(8,128)S(1)}, u32[]{:S(2)}, u32[]{:S(2)}) collective-permute-start(f32[16,16,256]{2,1,0:T(8,128)S(1)} %bitcast.285), channel_id=1, source_target_pairs={{0,3},{1,2},{2,1},{3,0},{4,7},{5,6},{6,5},{7,4},{8,11},{9,10},{10,... | collective-permute-start | bytes 786440 | tf_op jit(solution)/shard_map/ppermute | solution.py:28
  87.3 38.8 %collective-permute-start.7 = (f32[16,16,256]{2,1,0:T(8,128)S(1)}, f32[16,16,256]{2,1,0:T(8,128)S(1)}, u32[]{:S(2)}, u32[]{:S(2)}) collective-permute-start(f32[16,16,256]{2,1,0:T(8,128)S(1)} %bitcast.279), channel_id=1, source_target_pairs={{0,5},{1,4},{2,7},{3,6},{4,1},{5,0},{6,3},{7,2},{8,13},{9,12},{10,... | collective-permute-start | bytes 786440 | tf_op jit(solution)/shard_map/ppermute | solution.py:28
  91.4 35.5 %collective-permute-start.8 = (f32[16,16,256]{2,1,0:T(8,128)S(1)}, f32[16,16,256]{2,1,0:T(8,128)S(1)}, u32[]{:S(2)}, u32[]{:S(2)}) collective-permute-start(f32[16,16,256]{2,1,0:T(8,128)S(1)} %bitcast.276), channel_id=1, source_target_pairs={{0,6},{1,7},{2,4},{3,5},{4,2},{5,3},{6,0},{7,1},{8,14},{9,15},{10,... | collective-permute-start | bytes 786440 | tf_op jit(solution)/shard_map/ppermute | solution.py:28
  101.1 26.4 %collective-permute-start.9 = (f32[16,16,256]{2,1,0:T(8,128)S(1)}, f32[16,16,256]{2,1,0:T(8,128)S(1)}, u32[]{:S(2)}, u32[]{:S(2)}) collective-permute-start(f32[16,16,256]{2,1,0:T(8,128)S(1)} %bitcast.272), channel_id=1, source_target_pairs={{0,7},{1,6},{2,5},{3,4},{4,3},{5,2},{6,1},{7,0},{8,15},{9,14},{10,... | collective-permute-start | bytes 786440 | tf_op jit(solution)/shard_map/ppermute | solution.py:28
  213.4 63.3 %collective-permute-start.19 = (f32[2048]{0:T(1024)S(1)}, f32[2048]{0:T(1024)S(1)}, u32[]{:S(2)}, u32[]{:S(2)}) collective-permute-start(f32[2048]{0:T(1024)S(1)} %bitcast.298), channel_id=1, source_target_pairs={{8,0},{0,8},{9,1},{1,9},{10,2},{2,10},{11,3},{3,11},{12,4},{4,12},... | collective-permute-start | bytes 24584 | tf_op jit(solution)/shard_map/ppermute | solution.py:36
  213.4 70.2 %collective-permute-start.18 = (f32[16,128,128]{2,1,0:T(8,128)}, f32[16,128,128]{2,1,0:T(8,128)S(1)}, u32[]{:S(2)}, u32[]{:S(2)}) collective-permute-start(f32[16,128,128]{2,1,0:T(8,128)} %get-tuple-element.29), channel_id=1, source_target_pairs={{8,0},{0,8},{9,1},{1,9},{10,2},{2,10},{11,3},{3,11},{12,4},{4,12},... | collective-permute-start | bytes 3145736 | tf_op jit(solution)/shard_map/ppermute | solution.py:36
  215.2 18.4 %collective-permute-start.12 = (f32[16,16,256]{2,1,0:T(8,128)S(1)}, f32[16,16,256]{2,1,0:T(8,128)S(1)}, u32[]{:S(2)}, u32[]{:S(2)}) collective-permute-start(f32[16,16,256]{2,1,0:T(8,128)S(1)} %bitcast.294), channel_id=1, source_target_pairs={{0,3},{1,2},{2,1},{3,0},{4,7},{5,6},{6,5},{7,4},{8,11},{9,10},{10,... | collective-permute-start | bytes 786440 | tf_op jit(solution)/shard_map/ppermute | solution.py:28
  229.5 27.0 %collective-permute-start.14 = (f32[16,16,256]{2,1,0:T(8,128)S(1)}, f32[16,16,256]{2,1,0:T(8,128)S(1)}, u32[]{:S(2)}, u32[]{:S(2)}) collective-permute-start(f32[16,16,256]{2,1,0:T(8,128)S(1)} %bitcast.275), channel_id=1, source_target_pairs={{0,5},{1,4},{2,7},{3,6},{4,1},{5,0},{6,3},{7,2},{8,13},{9,12},{10,... | collective-permute-start | bytes 786440 | tf_op jit(solution)/shard_map/ppermute | solution.py:28
  233.6 23.7 %collective-permute-start.15 = (f32[16,16,256]{2,1,0:T(8,128)S(1)}, f32[16,16,256]{2,1,0:T(8,128)S(1)}, u32[]{:S(2)}, u32[]{:S(2)}) collective-permute-start(f32[16,16,256]{2,1,0:T(8,128)S(1)} %bitcast.271), channel_id=1, source_target_pairs={{0,6},{1,7},{2,4},{3,5},{4,2},{5,3},{6,0},{7,1},{8,14},{9,15},{10,... | collective-permute-start | bytes 786440 | tf_op jit(solution)/shard_map/ppermute | solution.py:28
  235.6 22.5 %collective-permute-start.16 = (f32[16,16,256]{2,1,0:T(8,128)S(1)}, f32[16,16,256]{2,1,0:T(8,128)S(1)}, u32[]{:S(2)}, u32[]{:S(2)}) collective-permute-start(f32[16,16,256]{2,1,0:T(8,128)S(1)} %bitcast.270), channel_id=1, source_target_pairs={{0,7},{1,6},{2,5},{3,4},{4,3},{5,2},{6,1},{7,0},{8,15},{9,14},{10,... | collective-permute-start | bytes 786440 | tf_op jit(solution)/shard_map/ppermute | solution.py:28
  264.1 19.1 %all-to-all-start.4 = ((f32[8,1,256]{2,1,0:T(1,128)}), f32[8,1,256]{2,1,0:T(1,128)S(1)}, u32[]{:S(2)}, u32[]{:S(2)}) async-start(f32[8,1,256]{2,1,0:T(1,128)} %broadcast_in_dim.10), calls=%async_computation.4 | async-start | bytes 16384 | tf_op jit(solution)/shard_map/all_to_all | solution.py:46
  288.6 51.6 %all-to-all-start.5 = ((f32[16,128,256]{2,0,1:T(8,128)}), f32[16,128,256]{2,0,1:T(8,128)}, u32[]{:S(2)}, u32[]{:S(2)}) async-start(f32[16,128,256]{2,0,1:T(8,128)} %copy.228), calls=%async_computation.5 | async-start | bytes 4194304 | tf_op jit(solution)/shard_map/all_to_all | solution.py:56
  293.2 49.0 %collective-permute-start.17 = (f32[16,128,128]{2,1,0:T(8,128)}, f32[16,128,128]{2,1,0:T(8,128)}, u32[]{:S(2)}, u32[]{:S(2)}) collective-permute-start(f32[16,128,128]{2,1,0:T(8,128)} %get-tuple-element.27), channel_id=1, source_target_pairs={{8,0},{0,8},{9,1},{1,9},{10,2},{2,10},{11,3},{3,11},{12,4},{4,12},... | collective-permute-start | bytes 3145736 | tf_op jit(solution)/shard_map/ppermute | solution.py:36
  346.8 19.9 %collective-permute-start.22 = (f32[16,16,256]{2,1,0:T(8,128)S(1)}, f32[16,16,256]{2,1,0:T(8,128)S(1)}, u32[]{:S(2)}, u32[]{:S(2)}) collective-permute-start(f32[16,16,256]{2,1,0:T(8,128)S(1)} %bitcast.286), channel_id=1, source_target_pairs={{0,3},{1,2},{2,1},{3,0},{4,7},{5,6},{6,5},{7,4},{8,11},{9,10},{10,... | collective-permute-start | bytes 786440 | tf_op jit(solution)/shard_map/ppermute | solution.py:28
  349.0 18.4 %collective-permute-start.23 = (f32[16,16,256]{2,1,0:T(8,128)S(1)}, f32[16,16,256]{2,1,0:T(8,128)S(1)}, u32[]{:S(2)}, u32[]{:S(2)}) collective-permute-start(f32[16,16,256]{2,1,0:T(8,128)S(1)} %bitcast.283), channel_id=1, source_target_pairs={{0,4},{1,5},{2,6},{3,7},{4,0},{5,1},{6,2},{7,3},{8,12},{9,13},{10,... | collective-permute-start | bytes 786440 | tf_op jit(solution)/shard_map/ppermute | solution.py:28
  349.6 38.7 %collective-permute-start.24 = (f32[16,16,256]{2,1,0:T(8,128)S(1)}, f32[16,16,256]{2,1,0:T(8,128)S(1)}, u32[]{:S(2)}, u32[]{:S(2)}) collective-permute-start(f32[16,16,256]{2,1,0:T(8,128)S(1)} %bitcast.280), channel_id=1, source_target_pairs={{0,5},{1,4},{2,7},{3,6},{4,1},{5,0},{6,3},{7,2},{8,13},{9,12},{10,... | collective-permute-start | bytes 786440 | tf_op jit(solution)/shard_map/ppermute | solution.py:28
  353.5 35.5 %collective-permute-start.25 = (f32[16,16,256]{2,1,0:T(8,128)S(1)}, f32[16,16,256]{2,1,0:T(8,128)S(1)}, u32[]{:S(2)}, u32[]{:S(2)}) collective-permute-start(f32[16,16,256]{2,1,0:T(8,128)S(1)} %bitcast.277), channel_id=1, source_target_pairs={{0,6},{1,7},{2,4},{3,5},{4,2},{5,3},{6,0},{7,1},{8,14},{9,15},{10,... | collective-permute-start | bytes 786440 | tf_op jit(solution)/shard_map/ppermute | solution.py:28
  363.3 26.4 %collective-permute-start.26 = (f32[16,16,256]{2,1,0:T(8,128)S(1)}, f32[16,16,256]{2,1,0:T(8,128)S(1)}, u32[]{:S(2)}, u32[]{:S(2)}) collective-permute-start(f32[16,16,256]{2,1,0:T(8,128)S(1)} %bitcast.273), channel_id=1, source_target_pairs={{0,7},{1,6},{2,5},{3,4},{4,3},{5,2},{6,1},{7,0},{8,15},{9,14},{10,... | collective-permute-start | bytes 786440 | tf_op jit(solution)/shard_map/ppermute | solution.py:28
  479.1 32.7 %collective-permute-start.30 = (f32[16,16,256]{2,1,0:T(8,128)S(1)}, f32[16,16,256]{2,1,0:T(8,128)S(1)}, u32[]{:S(2)}, u32[]{:S(2)}) collective-permute-start(f32[16,16,256]{2,1,0:T(8,128)S(1)} %bitcast.284), channel_id=1, source_target_pairs={{0,4},{1,5},{2,6},{3,7},{4,0},{5,1},{6,2},{7,3},{8,12},{9,13},{10,... | collective-permute-start | bytes 786440 | tf_op jit(solution)/shard_map/ppermute | solution.py:28
  480.4 38.0 %collective-permute-start.31 = (f32[16,16,256]{2,1,0:T(8,128)S(1)}, f32[16,16,256]{2,1,0:T(8,128)S(1)}, u32[]{:S(2)}, u32[]{:S(2)}) collective-permute-start(f32[16,16,256]{2,1,0:T(8,128)S(1)} %bitcast.281), channel_id=1, source_target_pairs={{0,5},{1,4},{2,7},{3,6},{4,1},{5,0},{6,3},{7,2},{8,13},{9,12},{10,... | collective-permute-start | bytes 786440 | tf_op jit(solution)/shard_map/ppermute | solution.py:28
  483.6 35.5 %collective-permute-start.32 = (f32[16,16,256]{2,1,0:T(8,128)S(1)}, f32[16,16,256]{2,1,0:T(8,128)S(1)}, u32[]{:S(2)}, u32[]{:S(2)}) collective-permute-start(f32[16,16,256]{2,1,0:T(8,128)S(1)} %bitcast.278), channel_id=1, source_target_pairs={{0,6},{1,7},{2,4},{3,5},{4,2},{5,3},{6,0},{7,1},{8,14},{9,15},{10,... | collective-permute-start | bytes 786440 | tf_op jit(solution)/shard_map/ppermute | solution.py:28
  491.3 28.5 %collective-permute-start.33 = (f32[16,16,256]{2,1,0:T(8,128)S(1)}, f32[16,16,256]{2,1,0:T(8,128)S(1)}, u32[]{:S(2)}, u32[]{:S(2)}) collective-permute-start(f32[16,16,256]{2,1,0:T(8,128)S(1)} %bitcast.274), channel_id=1, source_target_pairs={{0,7},{1,6},{2,5},{3,4},{4,3},{5,2},{6,1},{7,0},{8,15},{9,14},{10,... | collective-permute-start | bytes 786440 | tf_op jit(solution)/shard_map/ppermute | solution.py:28
  (24 other events, 216.5 us)
